TPU v7x, 32 devices: a whole 2x2x4 slice. The times are simulated.
32 devices in a mesh: shot: 4 (over x, core), rcv: 8 (over z, y).
Axes of the slice: x: 2, y: 2, z: 4, core: 2. Of those that a mesh axis runs over, the one named last changes fastest.
Arguments:
- response: bfloat16 [128, 128, 64], P('shot', 'rcv'), may hold values from -0.0625 to 0.0625
- traces: bfloat16 [128, 64, 512], P('shot', 'rcv'), may hold values from -6 to 6
Outputs:
- multiples: bfloat16 [128, 64, 512], P('shot', 'rcv')
All inputs are finite; a program needn't handle non-finite values.
Results may differ from a plain program's by a relative error of at most 0.001.
Values may be sent and summed in bfloat16 or wider, within the bound.
A program may use at most 256 MiB of HBM per device.

v0:
```python
import jax
import jax.numpy as jnp
from jax import lax
from jax.sharding import PartitionSpec as P


def banded(resp_piece):
    shots_here = resp_piece.shape[0]
    rows_in = resp_piece.shape[1]
    tap_count = resp_piece.shape[2]
    reversed_taps = jnp.transpose(resp_piece[:, :, ::-1], (2, 0, 1))
    lead = jnp.zeros((1, shots_here, rows_in), resp_piece.dtype)
    trail = jnp.zeros((tap_count, shots_here, rows_in), resp_piece.dtype)
    pattern = jnp.concatenate([lead, reversed_taps, trail], axis=0)
    repeated = jnp.tile(pattern, (tap_count, 1, 1))[: 2 * tap_count * tap_count]
    return repeated.reshape(tap_count, 2 * tap_count, shots_here, rows_in)


def contract(resp_piece, data_piece):
    shots_here = resp_piece.shape[0]
    tap_count = resp_piece.shape[2]
    rows_in = data_piece.shape[0]
    rcv_here = data_piece.shape[1]
    samples = data_piece.shape[2]
    blocks = samples // tap_count
    band = banded(resp_piece)
    padded = jnp.pad(data_piece, ((0, 0), (0, 0), (tap_count, 0)))
    tiles = padded.reshape(rows_in, rcv_here, blocks + 1, tap_count)
    windows = jnp.concatenate([tiles[:, :, :blocks], tiles[:, :, 1:]], axis=3)
    product = jnp.einsum("uvsk,krbv->srbu", band, windows, preferred_element_type=jnp.float32)
    return product.reshape(shots_here, rcv_here * samples)


def shards(response, traces):
    shots_here = response.shape[0]
    rcv_here = traces.shape[1]
    samples = traces.shape[2]
    responses_all = lax.all_gather(response, "rcv", axis=1, tiled=True)
    running = contract(responses_all, lax.all_gather(traces, "shot", axis=0, tiled=True))
    return running.reshape(shots_here, rcv_here, samples).astype(jnp.bfloat16)


def solution(mesh):
    placed = (P("shot", "rcv", None), P("shot", "rcv", None))
    return jax.shard_map(
        shards, mesh=mesh, in_specs=placed, out_specs=P("shot", "rcv", None), check_vma=False
    )
```

profile of v0, /device:TPU:0, one launch (start us, length us, event | category | flops | bytes accessed | tf_op | source)
XLA Modules:
  0.0 322.5 jit_solution(11808536504618366029)
XLA Ops:
  6.5 0.0 all-gather.2.cloned.1.call-start
  6.5 0.7 all-gather.2.cloned.1.call-update
  7.3 34.9 %all_gather.7 = bf16[32,128,64]{2,1,0:T(8,128)(2,1)S(1)} all-gather(bf16[32,16,64]{2,1,0:T(8,128)(2,1)} %param.2), channel_id=1, replica_groups=mesh['shot'=4,'rcv'=8] {'rcv'}, dimensions={1}, use_global_device_ids=true | all-gather | bytes 589824 | tf_op jit(solution)/shard_map/all_gather | solution.py:38
  42.1 2.9 rev.3
  45.0 0.1 pad.7.clone
  45.1 0.9 maximum_maximum_fusion
  46.0 1.3 copy.14
  47.3 28.0 %tile.4 = bf16[64,129,32,128]{3,2,1,0:T(8,128)(2,1)} broadcast(bf16[129,32,128]{2,1,0:T(8,128)(2,1)S(1)} %copy.14), dimensions={1,2,3} | broadcast | bytes 68689920 | tf_op jit(solution)/shard_map/tile | solution.py:15
  75.3 44.3 %slice.14 = bf16[8192,32,128]{2,1,0:T(8,128)(2,1)} slice(bf16[8256,32,128]{2,1,0:T(8,128)(2,1)} %bitcast.4), slice={[0:8192], [0:32], [0:128]} | slice | bytes 134217728 | tf_op jit(solution)/shard_map/slice | solution.py:15
  119.6 150.2 %copy.19 = bf16[64,128,32,128]{1,0,3,2:T(8,128)(2,1)} copy(bf16[64,128,32,128]{3,2,1,0:T(8,128)(2,1)} %bitcast.5) | data formatting | bytes 134217728 | tf_op jit(solution)/shard_map/reshape | solution.py:16
  269.8 0.0 all-gather.2.cloned.1.call-done
  269.8 1.9 copy.11
  271.7 0.1 pad.4
  271.8 0.5 fusion.14
  272.3 2.0 copy.21
  274.4 0.0 copy-start
  274.4 2.1 copy.20
  276.4 0.0 copy-done
  276.4 38.1 %fusion.10 = bf16[32,8,8,64]{3,2,0,1:T(8,128)(2,1)S(1)} fusion(bf16[64,128,32,128]{1,0,3,2:T(8,128)(2,1)} %copy.19, bf16[128,8,8,64]{3,2,0,1:T(8,128)(2,1)S(1)} %copy-done, bf16[128,8,8,64]{3,2,0,1:T(8,128)(2,1)} %copy.20), kind=kOutput, calls=%fused_computation.8 | convolution fusion | flops 4299292672 | bytes 69468160 | tf_op jit(solution)/shard_map/uvsk,krbv->srbu/dot_general | solution.py:30
  314.5 0.3 convert_element_type.13
  314.8 0.9 copy.16
  (2 shorter events, 0.0 us)
Async XLA Ops:
  6.5 263.3 %all-gather.2.cloned.1.call-start = ((), (), s32[]{:S(2)}) async-start(), calls=%async_computation | async-start | bytes 1310720 | tf_op jit(solution)/shard_map/all_gather | solution.py:39
  274.4 2.1 copy-start
Sparse Core Ops, SparseCore 0:
  8.9 19.4 all-gather.1
where the time goes:
time: 324 us; the launch traced here: 323 us
  local copies, waits for them, and re-layouts  235 us (73%)
  matrix products  38.1 us (12%)
  blocking collectives  34.9 us (11%)
  between operations  13.5 us (4%)
    reshape x1, local copies, waits for them, and re-layouts, banded(): return repeated.reshape(tap_count, 2 * tap_count, shots_here, rows_in)  150 us
    slice x1, local copies, waits for them, and re-layouts, banded(): repeated = jnp.tile(pattern, (tap_count, 1, 1))[:2 * tap_count * tap_count]  44.3 us
    dot_general x1, matrix products, contract(): jnp.einsum('uvsk,krbv->srbu', band, windows, preferred_element_type=jnp.f...  38.1 us
    all_gather x1, blocking collectives, shards(): responses_all = lax.all_gather(response, 'rcv', axis=1, tiled=True)  34.9 us
    another operation x1, local copies, waits for them, and re-layouts, banded(): repeated = jnp.tile(pattern, (tap_count, 1, 1))[:2 * tap_count * tap_count]  28 us
  transfers between devices with their start and end apart: 1, of which 0 were waited for; matrix products, arithmetic and copies ran while one was open for 71% of the time, Pallas kernels for 0%

commit v1 on v0

--- a/solution.py
+++ b/solution.py
@@ -2,6 +2,7 @@
 import jax.numpy as jnp
 from jax import lax
 from jax.sharding import PartitionSpec as P
+from jax.lax import all_to_all, axis_size
 
 
 def banded(resp_piece):
@@ -35,7 +36,8 @@
     shots_here = response.shape[0]
     rcv_here = traces.shape[1]
     samples = traces.shape[2]
-    responses_all = lax.all_gather(response, "rcv", axis=1, tiled=True)
+    wide_out = all_to_all(jnp.stack(axis_size("rcv") * [response]), "rcv", 0, 0)
+    responses_all = jnp.concatenate(wide_out, axis=1)
     running = contract(responses_all, lax.all_gather(traces, "shot", axis=0, tiled=True))
     return running.reshape(shots_here, rcv_here, samples).astype(jnp.bfloat16)
 

time: 324 us -> 314 us (0.969)
  blocking collectives: 34.9 us -> 0 us
  waiting for transfers between devices: 0.71 us -> 15.1 us
  starting transfers between devices: 0.01 us -> 7.31 us
    all_gather x1 -> x0, blocking collectives: 34.9 us -> none  [shards(): responses_all = lax.all_gather(response, 'rcv', axis=1, tiled=True)]
    all_to_all x0 -> x1, waiting for transfers between devices: none -> 14.4 us  [shards(): wide_out = all_to_all(jnp.stack(axis_size('rcv') * [response]), 'rcv', 0, 0)]
    all_to_all x0 -> x1, starting transfers between devices: none -> 7.31 us  [shards(): wide_out = all_to_all(jnp.stack(axis_size('rcv') * [response]), 'rcv', 0, 0)]
  transfers between devices with their start and end apart: 1 -> 2, of which waited for: 0 -> 1; matrix products, arithmetic and copies ran while one was open for 71% -> 74% of each run, Pallas kernels for 0% -> 0%
where the time goes in v1:
time: 314 us; the launch traced here: 313 us
  local copies, waits for them, and re-layouts  238 us (76%)
  matrix products  38.1 us (12%)
  waiting for transfers between devices  15.1 us (5%)
  between operations  13.5 us (4%)
  starting transfers between devices  7.31 us (2%)
    reshape x1, local copies, waits for them, and re-layouts, banded(): return repeated.reshape(tap_count, 2 * tap_count, shots_here, rows_in)  150 us
    slice x1, local copies, waits for them, and re-layouts, banded(): repeated = jnp.tile(pattern, (tap_count, 1, 1))[:2 * tap_count * tap_count]  44.3 us
    dot_general x1, matrix products, contract(): jnp.einsum('uvsk,krbv->srbu', band, windows, preferred_element_type=jnp.f...  38.1 us
    another operation x1, local copies, waits for them, and re-layouts, banded(): repeated = jnp.tile(pattern, (tap_count, 1, 1))[:2 * tap_count * tap_count]  28 us
    all_to_all x1, waiting for transfers between devices, shards(): wide_out = all_to_all(jnp.stack(axis_size('rcv') * [response]), 'rcv', 0, 0)  14.4 us
    all_to_all x1, starting transfers between devices, shards(): wide_out = all_to_all(jnp.stack(axis_size('rcv') * [response]), 'rcv', 0, 0)  7.31 us
  transfers between devices with their start and end apart: 2, of which 1 were waited for; matrix products, arithmetic and copies ran while one was open for 74% of the time, Pallas kernels for 0%

profile of v1, /device:TPU:0, one launch (start us, length us, event | category | flops | bytes accessed | tf_op | source)
XLA Modules:
  0.0 312.9 jit_solution(14104999835247984064)
XLA Ops:
  6.5 0.0 all-gather.2.cloned.1.call-start
  6.5 0.7 all-gather.2.cloned.1.call-update
  7.3 1.0 stack.2
  8.3 1.5 reshape.27
  9.8 7.3 %all-to-all-start = ((bf16[8,2,16384]{2,1,0:T(2,128)(2,1)}), bf16[8,2,16384]{2,1,0:T(2,128)(2,1)S(1)}, u32[]{:S(2)}, u32[]{:S(2)}) async-start(bf16[8,2,16384]{2,1,0:T(2,128)(2,1)} %reshape.27), calls=%async_computation | async-start | bytes 1048576 | tf_op jit(solution)/shard_map/all_to_all | solution.py:39
  17.1 0.1 pad.7.clone
  17.2 14.4 %all-to-all-done = bf16[8,2,16384]{2,1,0:T(2,128)(2,1)S(1)} async-done(((bf16[8,2,16384]{2,1,0:T(2,128)(2,1)}), bf16[8,2,16384]{2,1,0:T(2,128)(2,1)S(1)}, u32[]{:S(2)}, u32[]{:S(2)}) %all-to-all-start) | async-done | bytes 524320 | tf_op jit(solution)/shard_map/all_to_all | solution.py:39
  31.6 0.7 reshape.28
  32.3 0.3 copy.20
  32.6 2.9 rev.3
  35.5 0.9 maximum_maximum_fusion
  36.3 1.3 copy.21
  37.7 28.0 %tile.4 = bf16[64,129,32,128]{3,2,1,0:T(8,128)(2,1)} broadcast(bf16[129,32,128]{2,1,0:T(8,128)(2,1)S(1)} %copy.21), dimensions={1,2,3} | broadcast | bytes 68689920 | tf_op jit(solution)/shard_map/tile | solution.py:16
  65.6 44.3 %slice.14 = bf16[8192,32,128]{2,1,0:T(8,128)(2,1)} slice(bf16[8256,32,128]{2,1,0:T(8,128)(2,1)} %bitcast.6), slice={[0:8192], [0:32], [0:128]} | slice | bytes 134217728 | tf_op jit(solution)/shard_map/slice | solution.py:16
  109.9 150.2 %copy.26 = bf16[64,128,32,128]{1,0,3,2:T(8,128)(2,1)} copy(bf16[64,128,32,128]{3,2,1,0:T(8,128)(2,1)} %bitcast.7) | data formatting | bytes 134217728 | tf_op jit(solution)/shard_map/reshape | solution.py:17
  260.2 0.0 all-gather.2.cloned.1.call-done
  260.2 1.9 copy.17
  262.1 0.1 pad.4
  262.2 0.5 fusion.14
  262.7 2.0 copy.28
  264.7 0.0 copy-start
  264.7 2.0 copy.27
  266.8 0.0 copy-done
  266.8 38.1 %fusion.10 = bf16[32,8,8,64]{3,2,0,1:T(8,128)(2,1)S(1)} fusion(bf16[64,128,32,128]{1,0,3,2:T(8,128)(2,1)} %copy.26, bf16[128,8,8,64]{3,2,0,1:T(8,128)(2,1)S(1)} %copy-done, bf16[128,8,8,64]{3,2,0,1:T(8,128)(2,1)} %copy.27), kind=kOutput, calls=%fused_computation.8 | convolution fusion | flops 4299292672 | bytes 69468160 | tf_op jit(solution)/shard_map/uvsk,krbv->srbu/dot_general | solution.py:31
  304.9 0.3 convert_element_type.13
  305.2 0.9 copy.23
  (2 shorter events, 0.0 us)
Async XLA Ops:
  6.5 253.6 %all-gather.2.cloned.1.call-start = ((), (), s32[]{:S(2)}) async-start(), calls=%async_computation.1 | async-start | bytes 1310720 | tf_op jit(solution)/shard_map/all_gather | solution.py:41
  9.8 21.8 %all-to-all-start = ((bf16[8,2,16384]{2,1,0:T(2,128)(2,1)}), bf16[8,2,16384]{2,1,0:T(2,128)(2,1)S(1)}, u32[]{:S(2)}, u32[]{:S(2)}) async-start(bf16[8,2,16384]{2,1,0:T(2,128)(2,1)} %reshape.27), calls=%async_computation | async-start | bytes 1048576 | tf_op jit(solution)/shard_map/all_to_all | solution.py:39
  264.7 2.1 copy-start
Sparse Core Ops, SparseCore 0:
  8.9 19.4 all-gather.1
